TPU v7x, 32 devices: a whole 2x2x4 slice. The times are simulated.
32 devices in a mesh: dp: 8 (over y, x, core), tensor: 4 (over z).
Axes of the slice: x: 2, y: 2, z: 4, core: 2. Of those that a mesh axis runs over, the one named last changes fastest.
Arguments:
- activations: bfloat16 [8, 2048, 2048], P('dp', 'tensor'), may hold values from -6 to 6
- segment_ids: int32 [8, 2048], P('dp'), may hold values from 0 to 3, as said below
- attn_gain: float32 [2048], replicated, may hold values from 0.1 to 1.9
- w_query: bfloat16 [2048, 2048], P('dp', 'tensor'), may hold values from -0.125 to 0.125
- w_key: bfloat16 [2048, 512], P('dp', 'tensor'), may hold values from -0.125 to 0.125
- w_value: bfloat16 [2048, 512], P('dp', 'tensor'), may hold values from -0.125 to 0.125
- w_out: bfloat16 [2048, 2048], P('dp', 'tensor'), may hold values from -0.375 to 0.375
- mlp_gain: float32 [2048], replicated, may hold values from 0.1 to 1.9
- w_gate: bfloat16 [2048, 8192], P('dp', 'tensor'), may hold values from -0.125 to 0.125
- w_up: bfloat16 [2048, 8192], P('dp', 'tensor'), may hold values from -0.125 to 0.125
- w_down: bfloat16 [2048, 8192], P('dp', 'tensor'), may hold values from -0.09375 to 0.09375
- cotangent: bfloat16 [8, 2048, 2048], P('dp', 'tensor'), may hold values from -6 to 6
Outputs:
- output: bfloat16 [8, 2048, 2048], P('dp', 'tensor')
- input_grad: bfloat16 [8, 2048, 2048], P('dp', 'tensor')
- attn_gain_grad: float32 [2048], replicated
- w_query_grad: float32 [2048, 2048], P('dp', 'tensor')
- w_key_grad: float32 [2048, 512], P('dp', 'tensor')
- w_value_grad: float32 [2048, 512], P('dp', 'tensor')
- w_out_grad: float32 [2048, 2048], P('dp', 'tensor')
- mlp_gain_grad: float32 [2048], replicated
- w_gate_grad: float32 [2048, 8192], P('dp', 'tensor')
- w_up_grad: float32 [2048, 8192], P('dp', 'tensor')
- w_down_grad: float32 [2048, 8192], P('dp', 'tensor')
Inputs may be any that keep to these rules, and one draw needn't show every extreme that they name: `segment_ids`: along each sequence the ids never fall; each of the 4 documents has 204 to 1024 tokens, and exactly one document of each sequence has 1024.
All inputs are finite; a program needn't handle non-finite values.
Results may differ from a plain program's by a relative error of at most 0.018.
Values may be sent and summed in bfloat16 or wider, within the bound.
A program may use at most 320 MiB of HBM per device.

v0:
```python
import math
import jax
import jax.numpy as jnp
from jax import lax
from jax.sharding import PartitionSpec as P

HEAD_DIM = 64
DOCS = 4
QBLOCK = 512
NORM_EPS = 1e-05
ROPE_THETA = 500000.0


def matmul(left, right):
    return jnp.dot(left, right, preferred_element_type=jnp.float32)


def matmul_nt(left, right):
    return lax.dot_general(
        left, right, (((1,), (1,)), ((), ())), preferred_element_type=jnp.float32
    )


def matmul_tn(left, right):
    return lax.dot_general(
        left, right, (((0,), (0,)), ((), ())), preferred_element_type=jnp.float32
    )


def rope_tables(segments):
    length = segments.shape[-1]
    doc_ids = jnp.arange(DOCS, dtype=jnp.int32)
    member = (segments[..., :, None] == doc_ids).astype(jnp.int32)
    counts = jnp.sum(member, axis=-2)
    before = (doc_ids < segments[..., :, None]).astype(jnp.int32)
    first = jnp.sum(before * counts[..., None, :], axis=-1)
    position = (jnp.arange(length, dtype=jnp.int32) - first).astype(jnp.float32)
    frequency = jnp.exp(
        jnp.arange(HEAD_DIM // 2, dtype=jnp.float32) * (-2.0 * math.log(ROPE_THETA) / HEAD_DIM)
    )
    angles = position[..., None] * frequency
    return (jnp.cos(angles), jnp.sin(angles))


def rotate(values_in, cosine, sine_tab):
    half_dim = HEAD_DIM // 2
    first_half = values_in[..., :half_dim]
    second_half = values_in[..., half_dim:]
    cos_wide = cosine[..., None, :]
    sin_wide = sine_tab[..., None, :]
    return jnp.concatenate(
        [
            first_half * cos_wide - second_half * sin_wide,
            second_half * cos_wide + first_half * sin_wide,
        ],
        axis=-1,
    )


def rotate_back(grad_in, cosine, sine_tab):
    half_dim = HEAD_DIM // 2
    first_half = grad_in[..., :half_dim]
    second_half = grad_in[..., half_dim:]
    cos_wide = cosine[..., None, :]
    sin_wide = sine_tab[..., None, :]
    return jnp.concatenate(
        [
            first_half * cos_wide + second_half * sin_wide,
            second_half * cos_wide - first_half * sin_wide,
        ],
        axis=-1,
    )


def rms_scale(values_in):
    return lax.rsqrt(jnp.mean(values_in * values_in, axis=-1, keepdims=True) + NORM_EPS)


def norm_back(values_in, scaling, gain, grad_in):
    gained = grad_in * gain
    gain_part = jnp.sum(grad_in * values_in * scaling, axis=(0, 1))
    inner = jnp.mean(gained * values_in, axis=-1, keepdims=True)
    return (gain_part, scaling * gained - values_in * scaling * scaling * scaling * inner)


def gather_rows(local_rows):
    return lax.all_gather(local_rows, "tensor", axis=1, tiled=True)


def sum_rows(partial_rows):
    return lax.psum_scatter(partial_rows, "tensor", scatter_dimension=1, tiled=True)


def block_inputs(block_id, query_rot, key_rot, value_rows, segment_ids):
    length = segment_ids.shape[1]
    blocks = length // QBLOCK
    seq_id = block_id // blocks
    offset = block_id % blocks * QBLOCK
    query_seq = lax.dynamic_index_in_dim(query_rot, seq_id, 0, False)
    query_block = lax.dynamic_slice_in_dim(query_seq, offset, QBLOCK, 0)
    key_seq = lax.dynamic_index_in_dim(key_rot, seq_id, 0, False)
    value_seq = lax.dynamic_index_in_dim(value_rows, seq_id, 0, False)
    seg_seq = lax.dynamic_index_in_dim(segment_ids, seq_id, 0, False)
    query_seg = lax.dynamic_slice_in_dim(seg_seq, offset, QBLOCK, 0)
    query_pos = offset + jnp.arange(QBLOCK, dtype=jnp.int32)
    key_pos = jnp.arange(length, dtype=jnp.int32)
    allowed = (query_seg[:, None] == seg_seq[None, :]) & (key_pos[None, :] <= query_pos[:, None])
    score = jnp.einsum(
        "qkgd,skd->kgqs", query_block, key_seq, preferred_element_type=jnp.float32
    ) * HEAD_DIM ** (-0.5)
    score = jnp.where(allowed, score, -1e30)
    return (seq_id, offset, query_block, key_seq, value_seq, score)


def attend(query_rot, key_rot, value_rows, segment_ids):
    seq_count, length = segment_ids.shape

    def one_block(block_id):
        seq_id, offset, query_block, key_seq, value_seq, score = block_inputs(
            block_id, query_rot, key_rot, value_rows, segment_ids
        )
        row_max = jnp.max(score, axis=-1, keepdims=True)
        expd = jnp.exp(score - row_max)
        row_sum = jnp.sum(expd, axis=-1, keepdims=True)
        weights = (expd / row_sum).astype(jnp.bfloat16)
        result = jnp.einsum(
            "kgqs,skd->qkgd", weights, value_seq, preferred_element_type=jnp.float32
        ).astype(jnp.bfloat16)
        return (result, row_max[..., 0] + jnp.log(row_sum[..., 0]))

    count_blocks = seq_count * (length // QBLOCK)
    results, log_sums = lax.map(one_block, jnp.arange(count_blocks, dtype=jnp.int32))
    return (results.reshape(seq_count, length, *results.shape[2:]), log_sums)


def attend_back(query_rot, key_rot, value_rows, grad_att, log_sums, segment_ids):
    seq_count, length = segment_ids.shape
    blocks = length // QBLOCK

    def one_block(block_id):
        seq_id, offset, query_block, key_seq, value_seq, score = block_inputs(
            block_id, query_rot, key_rot, value_rows, segment_ids
        )
        grad_seq = lax.dynamic_index_in_dim(grad_att, seq_id, 0, False)
        grad_block = lax.dynamic_slice_in_dim(grad_seq, offset, QBLOCK, 0)
        lse_block = lax.dynamic_index_in_dim(log_sums, block_id, 0, False)
        prob_rows = jnp.exp(score - lse_block[..., None])
        weights = prob_rows.astype(jnp.bfloat16)
        grad_weights = jnp.einsum(
            "qkgd,skd->kgqs", grad_block, value_seq, preferred_element_type=jnp.float32
        )
        row_dot = jnp.sum(grad_weights * prob_rows, axis=-1, keepdims=True)
        grad_score = (prob_rows * (grad_weights - row_dot)).astype(jnp.bfloat16)
        scaling = HEAD_DIM ** (-0.5)
        grad_query = (
            jnp.einsum("kgqs,skd->qkgd", grad_score, key_seq, preferred_element_type=jnp.float32)
            * scaling
        )
        grad_key = (
            jnp.einsum(
                "kgqs,qkgd->skd", grad_score, query_block, preferred_element_type=jnp.float32
            )
            * scaling
        )
        grad_value = jnp.einsum(
            "kgqs,qkgd->skd", weights, grad_block, preferred_element_type=jnp.float32
        )
        return (grad_query, grad_key, grad_value)

    grad_query, grad_key, grad_value = lax.map(
        one_block, jnp.arange(seq_count * blocks, dtype=jnp.int32)
    )
    grad_query = grad_query.reshape(seq_count, length, *grad_query.shape[2:])
    grad_key = jnp.sum(grad_key.reshape(seq_count, blocks, length, *grad_key.shape[2:]), axis=1)
    grad_value = jnp.sum(
        grad_value.reshape(seq_count, blocks, length, *grad_value.shape[2:]), axis=1
    )
    return (grad_query, grad_key, grad_value)


def per_device(
    activations,
    segment_ids,
    attn_gain,
    w_query,
    w_key,
    w_value,
    w_out,
    mlp_gain,
    w_gate,
    w_up,
    w_down,
    cotangent,
):
    seq_count, row_count, model_width = activations.shape
    length = segment_ids.shape[1]
    tok_count = seq_count * length
    kv_local = w_key.shape[1] // HEAD_DIM
    head_local = w_query.shape[1] // HEAD_DIM
    group_size = head_local // kv_local
    cosine, sine_tab = rope_tables(segment_ids)
    attn_full = (
        lax.all_gather(w_query, "dp", axis=0, tiled=True),
        lax.all_gather(w_key, "dp", axis=0, tiled=True),
        lax.all_gather(w_value, "dp", axis=0, tiled=True),
        lax.all_gather(w_out, "dp", axis=0, tiled=True),
    )
    x_float = activations.astype(jnp.float32)
    scale_one = rms_scale(x_float)
    normed = gather_rows((x_float * scale_one * attn_gain).astype(jnp.bfloat16)).reshape(
        tok_count, model_width
    )
    query_rot = rotate(
        matmul(normed, attn_full[0]).reshape(seq_count, length, head_local, HEAD_DIM),
        cosine,
        sine_tab,
    )
    query_rot = query_rot.astype(jnp.bfloat16).reshape(
        seq_count, length, kv_local, group_size, HEAD_DIM
    )
    key_rot = rotate(
        matmul(normed, attn_full[1]).reshape(seq_count, length, kv_local, HEAD_DIM),
        cosine,
        sine_tab,
    ).astype(jnp.bfloat16)
    value_rows = (
        matmul(normed, attn_full[2])
        .astype(jnp.bfloat16)
        .reshape(seq_count, length, kv_local, HEAD_DIM)
    )
    attended, log_sums = attend(query_rot, key_rot, value_rows, segment_ids)
    attended_flat = attended.reshape(tok_count, head_local * HEAD_DIM)
    resid = x_float + sum_rows(
        matmul_nt(attended_flat, attn_full[3]).reshape(seq_count, length, model_width)
    )
    mlp_full = (
        lax.all_gather(w_gate, "dp", axis=0, tiled=True),
        lax.all_gather(w_up, "dp", axis=0, tiled=True),
        lax.all_gather(w_down, "dp", axis=0, tiled=True),
    )
    scale_two = rms_scale(resid)
    normed_mlp = gather_rows((resid * scale_two * mlp_gain).astype(jnp.bfloat16)).reshape(
        tok_count, model_width
    )
    gate_pre = matmul(normed_mlp, mlp_full[0])
    up_proj = matmul(normed_mlp, mlp_full[1])
    hidden = (jax.nn.silu(gate_pre) * up_proj).astype(jnp.bfloat16)
    output = (
        resid + sum_rows(matmul_nt(hidden, mlp_full[2]).reshape(seq_count, length, model_width))
    ).astype(jnp.bfloat16)
    mlp_back = (
        lax.all_gather(w_gate, "dp", axis=0, tiled=True),
        lax.all_gather(w_up, "dp", axis=0, tiled=True),
        lax.all_gather(w_down, "dp", axis=0, tiled=True),
    )
    grad_full = gather_rows(cotangent).reshape(tok_count, model_width)
    grad_down_w = matmul_tn(grad_full, hidden)
    grad_hidden = matmul(grad_full, mlp_back[2])
    sigma = jax.nn.sigmoid(gate_pre)
    grad_gate = (grad_hidden * up_proj * sigma * (1.0 + gate_pre * (1.0 - sigma))).astype(
        jnp.bfloat16
    )
    grad_up = (grad_hidden * gate_pre * sigma).astype(jnp.bfloat16)
    grad_gate_w = matmul_tn(normed_mlp, grad_gate)
    grad_up_w = matmul_tn(normed_mlp, grad_up)
    grad_normed_mlp = matmul_nt(grad_gate, mlp_back[0]) + matmul_nt(grad_up, mlp_back[1])
    grad_normed_mlp = sum_rows(grad_normed_mlp.reshape(seq_count, length, model_width))
    gain_two_part, grad_resid_norm = norm_back(resid, scale_two, mlp_gain, grad_normed_mlp)
    grad_resid = cotangent.astype(jnp.float32) + grad_resid_norm
    attn_back = (
        lax.all_gather(w_query, "dp", axis=0, tiled=True),
        lax.all_gather(w_key, "dp", axis=0, tiled=True),
        lax.all_gather(w_value, "dp", axis=0, tiled=True),
        lax.all_gather(w_out, "dp", axis=0, tiled=True),
    )
    grad_resid_full = gather_rows(grad_resid.astype(jnp.bfloat16)).reshape(tok_count, model_width)
    grad_out_w = matmul_tn(grad_resid_full, attended_flat)
    grad_att = matmul(grad_resid_full, attn_back[3]).astype(jnp.bfloat16)
    grad_att = grad_att.reshape(seq_count, length, kv_local, group_size, HEAD_DIM)
    grad_query_rot, grad_key_rot, grad_value_rows = attend_back(
        query_rot, key_rot, value_rows, grad_att, log_sums, segment_ids
    )
    grad_query = rotate_back(
        grad_query_rot.reshape(seq_count, length, head_local, HEAD_DIM), cosine, sine_tab
    )
    grad_query = grad_query.astype(jnp.bfloat16).reshape(tok_count, head_local * HEAD_DIM)
    grad_key = (
        rotate_back(grad_key_rot, cosine, sine_tab)
        .astype(jnp.bfloat16)
        .reshape(tok_count, kv_local * HEAD_DIM)
    )
    grad_value = grad_value_rows.astype(jnp.bfloat16).reshape(tok_count, kv_local * HEAD_DIM)
    grad_query_w = matmul_tn(normed, grad_query)
    grad_key_w = matmul_tn(normed, grad_key)
    grad_value_w = matmul_tn(normed, grad_value)
    grad_normed = (
        matmul_nt(grad_query, attn_back[0])
        + matmul_nt(grad_key, attn_back[1])
        + matmul_nt(grad_value, attn_back[2])
    )
    grad_normed = sum_rows(grad_normed.reshape(seq_count, length, model_width))
    gain_one_part, grad_x_norm = norm_back(x_float, scale_one, attn_gain, grad_normed)
    input_grad = (grad_resid + grad_x_norm).astype(jnp.bfloat16)
    gain_totals = lax.psum((gain_one_part, gain_two_part), ("dp", "tensor"))
    all_sums = (
        lax.psum_scatter(
            grad_query_w.astype(jnp.bfloat16), "dp", scatter_dimension=0, tiled=True
        ).astype(jnp.float32),
        lax.psum_scatter(
            grad_key_w.astype(jnp.bfloat16), "dp", scatter_dimension=0, tiled=True
        ).astype(jnp.float32),
        lax.psum_scatter(
            grad_value_w.astype(jnp.bfloat16), "dp", scatter_dimension=0, tiled=True
        ).astype(jnp.float32),
        lax.psum_scatter(
            grad_out_w.astype(jnp.bfloat16), "dp", scatter_dimension=0, tiled=True
        ).astype(jnp.float32),
        lax.psum_scatter(
            grad_gate_w.astype(jnp.bfloat16), "dp", scatter_dimension=0, tiled=True
        ).astype(jnp.float32),
        lax.psum_scatter(
            grad_up_w.astype(jnp.bfloat16), "dp", scatter_dimension=0, tiled=True
        ).astype(jnp.float32),
        lax.psum_scatter(
            grad_down_w.astype(jnp.bfloat16), "dp", scatter_dimension=0, tiled=True
        ).astype(jnp.float32),
    )
    attn_sums = all_sums[:4]
    mlp_sums = all_sums[4:]
    return (
        output,
        input_grad,
        gain_totals[0],
        attn_sums[0],
        attn_sums[1],
        attn_sums[2],
        attn_sums[3],
        gain_totals[1],
        mlp_sums[0],
        mlp_sums[1],
        mlp_sums[2],
    )


def solution(mesh):
    in_specs = (
        P("dp", "tensor", None),
        P("dp", None),
        P(),
        P("dp", "tensor"),
        P("dp", "tensor"),
        P("dp", "tensor"),
        P("dp", "tensor"),
        P(),
        P("dp", "tensor"),
        P("dp", "tensor"),
        P("dp", "tensor"),
        P("dp", "tensor", None),
    )
    out_specs = (
        P("dp", "tensor", None),
        P("dp", "tensor", None),
        P(),
        P("dp", "tensor"),
        P("dp", "tensor"),
        P("dp", "tensor"),
        P("dp", "tensor"),
        P(),
        P("dp", "tensor"),
        P("dp", "tensor"),
        P("dp", "tensor"),
    )
    return jax.shard_map(
        per_device, mesh=mesh, in_specs=in_specs, out_specs=out_specs, check_vma=False
    )
```

profile of v0, /device:TPU:0, one launch (start us, length us, event | category | flops | bytes accessed | tf_op | source)
XLA Modules:
  0.0 2988.1 jit_solution(1791326415638827385)
XLA Ops:
  45.6 149.2 %all-gather.10.cloned.1.call-done = bf16[1,2048,2048]{2,1,0:T(8,128)(2,1)} async-done(((bf16[1,512,2048]{2,1,0:T(8,128)(2,1)}), bf16[1,2048,2048]{2,1,0:T(8,128)(2,1)}) %all-gather.10.cloned.1.call-update) | async-done | bytes 8388624 | tf_op jit(solution)/shard_map/all_gather | solution.py:87
  211.1 199.4 %while.30 = (s32[]{:T(128)}, bf16[4,512,2,4,64]{1,4,3,2,0:T(8,128)(2,1)}, f32[4,2,4,512]{3,2,1,0:T(4,128)}, s32[4]{0:T(128)S(1)}, s32[1,2048]{1,0:T(1,128)S(1)},...) while((s32[]{:T(128)}, ...), condition=%wide.region_6.7_spmd, body=%wide.region_3.6_spmd.sunk | while | flops 2251551232 | bytes 107104584 | solution.py:132
  429.4 278.2 %reduce-scatter.12.cloned.1.call-done = f32[1,512,2048]{2,1,0:T(8,128)} async-done(((f32[1,2048,2048]{2,1,0:T(8,128)}), f32[1,512,2048]{2,1,0:T(8,128)}) %reduce-scatter.12.cloned.1.call-update) | async-done | bytes 4194320 | tf_op jit(solution)/shard_map/reduce_scatter | solution.py:91
  716.5 48.2 %all-gather.20.cloned.1.call-done = bf16[2048,2048]{1,0:T(8,128)(2,1)} async-done(((bf16[256,2048]{1,0:T(8,128)(2,1)}), bf16[2048,2048]{1,0:T(8,128)(2,1)}) %all-gather.20.cloned.1.call-update) | async-done | bytes 8388624 | tf_op jit(solution)/shard_map/all_gather | solution.py:238
  764.6 151.7 %all-gather.16.cloned.1.call-done = bf16[1,2048,2048]{2,1,0:T(8,128)(2,1)} async-done(((bf16[1,512,2048]{2,1,0:T(8,128)(2,1)}), bf16[1,2048,2048]{2,1,0:T(8,128)(2,1)}) %all-gather.16.cloned.1.call-update) | async-done | bytes 8388624 | tf_op jit(solution)/shard_map/all_gather | solution.py:87
  940.7 30.3 %all-gather.18.cloned.1.call-done = bf16[2048,2048]{1,0:T(8,128)(2,1)} async-done(((bf16[256,2048]{1,0:T(8,128)(2,1)}), bf16[2048,2048]{1,0:T(8,128)(2,1)}) %all-gather.18.cloned.1.call-update) | async-done | bytes 8388624 | tf_op jit(solution)/shard_map/all_gather | solution.py:237
  995.3 127.1 %all-gather.24.cloned.1.call-done = bf16[1,2048,2048]{2,1,0:T(8,128)(2,1)} async-done(((bf16[1,512,2048]{2,1,0:T(8,128)(2,1)}), bf16[1,2048,2048]{2,1,0:T(8,128)(2,1)}) %all-gather.24.cloned.1.call-update) | async-done | bytes 8388624 | tf_op jit(solution)/shard_map/all_gather | solution.py:87
  1122.4 54.7 %all-gather.22.cloned.1.call-done = bf16[2048,2048]{1,0:T(8,128)(2,1)} async-done(((bf16[256,2048]{1,0:T(8,128)(2,1)}), bf16[2048,2048]{1,0:T(8,128)(2,1)}) %all-gather.22.cloned.1.call-update) | async-done | bytes 8388624 | tf_op jit(solution)/shard_map/all_gather | solution.py:239
  1177.1 34.8 %multiply_convert_fusion = (bf16[2048,2048]{1,0:T(8,128)(2,1)}, bf16[2048,2048]{1,0:T(8,128)(2,1)}, bf16[2048,2048]{1,0:T(8,128)(2,1)}) fusion(f32[2048,2048]{1,0:T(8,128)} %fusion.67, f32[2048,2048]{1,0:T(8,128)} %fusion.65, bf16[2048,2048]{1,0:T(8,128)(2,1)} %all-gather.22.cloned.1.call-done, bf16[1,2048,2048]{2,1,0:T(8,128)(2,1)} %all-gather.24.cloned.1.call-done), kind=kOutput, calls=%fused_computation.67 | convolution fusion | flops 17246978048 | bytes 75497472 | tf_op jit(solution)/shard_map/dot_general | solution.py:15
  1236.2 26.7 add_bitcast_fusion.1
  1263.0 280.4 %reduce-scatter.16.cloned.1.call-done = f32[1,512,2048]{2,1,0:T(8,128)} async-done(((f32[1,2048,2048]{2,1,0:T(8,128)}), f32[1,512,2048]{2,1,0:T(8,128)}) %reduce-scatter.16.cloned.1.call-update) | async-done | bytes 4194320 | tf_op jit(solution)/shard_map/reduce_scatter | solution.py:91
  1624.0 78.7 %all-gather.26.cloned.1.call-done = bf16[1,2048,2048]{2,1,0:T(8,128)(2,1)} async-done(((bf16[1,512,2048]{2,1,0:T(8,128)(2,1)}), bf16[1,2048,2048]{2,1,0:T(8,128)(2,1)}) %all-gather.26.cloned.1.call-update) | async-done | bytes 8388624 | tf_op jit(solution)/shard_map/all_gather | solution.py:87
  1712.6 521.1 %while.31 = (s32[]{:T(128)}, f32[4,512,2,4,64]{1,0,4,3,2:T(4,128)}, f32[4,2048,2,64]{1,3,2,0:T(8,128)}, f32[4,2048,2,64]{1,3,2,0:T(8,128)}, s32[4]{0:T(128)S(1)}...) while((s32[]{:T(128)}, f32[4,512,2,4,64]{1,0,4,3,2:T(4,128)}, ...), condition=%wide.region_14.15_spmd, body=%wide.region_12.14_spmd.sunk | while | flops 5498204672 | bytes 367659456 | solution.py:170
  1750.0 26.5 fusion.192
  1776.5 31.1 %fusion.193 = bf16[2,4,512,2048]{3,2,1,0:T(8,128)(2,1)} fusion(f32[2,512,4,2048]{3,1,2,0:T(8,128)} %get-tuple-element.479, f32[2,512,4,2048]{3,1,2,0:T(8,128)} %fusion.190, f32[2,4,512]{2,1,0:T(4,128)S(1)} %get-tuple-element.480, f32[2,4,512]{2,1,0:T(4,128)S(1)} %dynamic-slice_bitcast_fusion.2, pred[512,2048]{1,0:T(8,128)(4,1)S(1)} %fusion.191), kind=kLoop, calls=%fused_computation.27.clone.1 | loop fusion | flops 50331648 | bytes 84967424 | tf_op jit(solution)/shard_map/while/body/eval_jaxpr/convert_element_type | solution.py:153
  1886.3 26.4 fusion.192
  1912.8 28.3 fusion.193
  2014.3 26.3 fusion.192
  2040.6 27.7 fusion.193
  2167.8 27.7 fusion.193
  2360.8 43.2 %reduce-scatter.20.cloned.1.call-done = bf16[256,512]{1,0:T(8,128)(2,1)} async-done(((bf16[2048,512]{1,0:T(8,128)(2,1)}), bf16[256,512]{1,0:T(8,128)(2,1)}) %reduce-scatter.20.cloned.1.call-update) | async-done | bytes 262160 | tf_op jit(solution)/shard_map/reduce_scatter | solution.py:306
  2405.8 281.0 %reduce-scatter.18.cloned.1.call-done = f32[1,512,2048]{2,1,0:T(8,128)} async-done(((f32[1,2048,2048]{2,1,0:T(8,128)}), f32[1,512,2048]{2,1,0:T(8,128)}) %reduce-scatter.18.cloned.1.call-update) | async-done | bytes 4194320 | tf_op jit(solution)/shard_map/reduce_scatter | solution.py:91
  2690.3 46.1 %all-reduce = (f32[2048]{0:T(1024)}, f32[2048]{0:T(1024)}) all-reduce(f32[2048]{0:T(1024)S(1)} %get-tuple-element.294, f32[2048]{0:T(1024)S(1)} %copy-done.38), channel_id=1, replica_groups=mesh['dp'=8,'tensor'=4] {'dp','tensor'}, use_global_device_ids=true, to_apply=%region_20.21 | all-reduce | flops 4096 | bytes 32768 | tf_op jit(solution)/shard_map/psum | solution.py:304
  2736.4 234.7 %reduce-scatter.14.cloned.1.call-done = f32[1,512,2048]{2,1,0:T(8,128)} async-done(((f32[1,2048,2048]{2,1,0:T(8,128)}), f32[1,512,2048]{2,1,0:T(8,128)}) %reduce-scatter.14.cloned.1.call-update) | async-done | bytes 4194320 | tf_op jit(solution)/shard_map/reduce_scatter | solution.py:91
  (292 shorter events, 891.2 us)
Async XLA Ops:
  7.2 35.5 %all-gather.12.cloned.1.call-start = ((), (), s32[]{:S(2)}) async-start(), calls=%async_computation.12 | async-start | bytes 2359296 | tf_op jit(solution)/shard_map/all_gather | solution.py:203
  7.9 186.9 %all-gather.10.cloned.1.call-start = ((), (), s32[]{:S(2)}) async-start(), calls=%async_computation.11 | async-start | bytes 10485760 | tf_op jit(solution)/shard_map/all_gather | solution.py:87
  13.6 402.6 %all-gather.14.cloned.1.call-start = ((), (), s32[]{:S(2)}) async-start(), calls=%async_computation.13 | async-start | bytes 2359296 | tf_op jit(solution)/shard_map/all_gather | solution.py:206
  14.3 693.3 %reduce-scatter.12.cloned.1.call-start = ((), (), s32[]{:S(2)}) async-start(), calls=%async_computation.14 | async-start | bytes 20971520 | tf_op jit(solution)/shard_map/reduce_scatter | solution.py:91
  428.7 335.9 %all-gather.20.cloned.1.call-start = ((), (), s32[]{:S(2)}) async-start(), calls=%async_computation.17 | async-start | bytes 9437184 | tf_op jit(solution)/shard_map/all_gather | solution.py:238
  429.3 487.0 %all-gather.16.cloned.1.call-start = ((), (), s32[]{:S(2)}) async-start(), calls=%async_computation.15 | async-start | bytes 10485760 | tf_op jit(solution)/shard_map/all_gather | solution.py:87
  714.2 256.9 %all-gather.18.cloned.1.call-start = ((), (), s32[]{:S(2)}) async-start(), calls=%async_computation.16 | async-start | bytes 9437184 | tf_op jit(solution)/shard_map/all_gather | solution.py:237
  714.9 407.5 %all-gather.24.cloned.1.call-start = ((), (), s32[]{:S(2)}) async-start(), calls=%async_computation.20 | async-start | bytes 10485760 | tf_op jit(solution)/shard_map/all_gather | solution.py:87
  715.7 461.4 %all-gather.22.cloned.1.call-start = ((), (), s32[]{:S(2)}) async-start(), calls=%async_computation.18 | async-start | bytes 9437184 | tf_op jit(solution)/shard_map/all_gather | solution.py:239
  716.4 827.0 %reduce-scatter.16.cloned.1.call-start = ((), (), s32[]{:S(2)}) async-start(), calls=%async_computation.21 | async-start | bytes 20971520 | tf_op jit(solution)/shard_map/reduce_scatter | solution.py:91
  1262.9 439.8 %all-gather.26.cloned.1.call-start = ((), (), s32[]{:S(2)}) async-start(), calls=%async_computation.22 | async-start | bytes 10485760 | tf_op jit(solution)/shard_map/all_gather | solution.py:87
  1552.2 790.1 %reduce-scatter.32.cloned.1.call-start = ((), (), s32[]{:S(2)}) async-start(), calls=%async_computation.30 | async-start | bytes 9437184 | tf_op jit(solution)/shard_map/reduce_scatter | solution.py:324
  1576.0 768.8 %reduce-scatter.30.cloned.1.call-start = ((), (), s32[]{:S(2)}) async-start(), calls=%async_computation.29 | async-start | bytes 9437184 | tf_op jit(solution)/shard_map/reduce_scatter | solution.py:321
  1600.0 747.8 %reduce-scatter.28.cloned.1.call-start = ((), (), s32[]{:S(2)}) async-start(), calls=%async_computation.28 | async-start | bytes 9437184 | tf_op jit(solution)/shard_map/reduce_scatter | solution.py:318
  1624.0 726.7 %reduce-scatter.22.cloned.1.call-start = ((), (), s32[]{:S(2)}) async-start(), calls=%async_computation.25 | async-start | bytes 589824 | tf_op jit(solution)/shard_map/reduce_scatter | solution.py:309
  2243.2 108.9 %reduce-scatter.24.cloned.1.call-start = ((), (), s32[]{:S(2)}) async-start(), calls=%async_computation.26 | async-start | bytes 589824 | tf_op jit(solution)/shard_map/reduce_scatter | solution.py:312
  2252.6 106.5 %reduce-scatter.26.cloned.1.call-start = ((), (), s32[]{:S(2)}) async-start(), calls=%async_computation.27 | async-start | bytes 2359296 | tf_op jit(solution)/shard_map/reduce_scatter | solution.py:315
  2262.6 141.4 %reduce-scatter.20.cloned.1.call-start = ((), (), s32[]{:S(2)}) async-start(), calls=%async_computation.24 | async-start | bytes 2359296 | tf_op jit(solution)/shard_map/reduce_scatter | solution.py:306
  2282.9 404.0 %reduce-scatter.18.cloned.1.call-start = ((), (), s32[]{:S(2)}) async-start(), calls=%async_computation.23 | async-start | bytes 20971520 | tf_op jit(solution)/shard_map/reduce_scatter | solution.py:91
  2317.5 653.5 %reduce-scatter.14.cloned.1.call-start = ((), (), s32[]{:S(2)}) async-start(), calls=%async_computation.19 | async-start | bytes 20971520 | tf_op jit(solution)/shard_map/reduce_scatter | solution.py:91
  2344.8 342.0 %copy-start.37 = (f32[512]{0:T(512)S(1)}, f32[512]{0:T(512)}, u32[]{:S(2)}) copy-start(f32[512]{0:T(512)} %copy-done.36) | copy-start | bytes 6148
  2350.6 620.5 %copy-start.29 = (f32[2048]{0:T(1024)S(1)}, f32[2048]{0:T(1024)}, u32[]{:S(2)}) copy-start(f32[2048]{0:T(1024)} %param.23) | copy-start | bytes 24580
  2350.6 620.5 %copy-start.35 = (f32[512]{0:T(512)S(1)}, f32[512]{0:T(512)}, u32[]{:S(2)}) copy-start(f32[512]{0:T(512)} %copy-done.33) | copy-start | bytes 6148
  2350.6 620.5 %copy-start.40 = (f32[512]{0:T(512)S(1)}, f32[512]{0:T(512)}, u32[]{:S(2)}) copy-start(f32[512]{0:T(512)} %copy-done.39) | copy-start | bytes 6148
  (46 other events, 3535.2 us)
Sparse Core Ops, SparseCore 0:
  9.9 32.7 all-gather.11
  44.8 149.9 all-gather.9
  196.7 26.1 all-gather.13
  428.8 278.6 reduce-scatter.11
  709.5 55.1 all-gather.19
  766.7 149.6 all-gather.15
  918.4 52.6 all-gather.17
  972.7 149.6 all-gather.23
  1124.4 52.6 all-gather.21
  1263.1 280.2 reduce-scatter.15
  1552.3 150.3 all-gather.25
  1706.0 69.5 reduce-scatter.31
  1779.5 71.2 reduce-scatter.29
  1854.1 71.2 reduce-scatter.27
  2243.4 32.6 reduce-scatter.21
  2279.6 34.1 reduce-scatter.23
  2317.8 41.2 reduce-scatter.25
  2362.8 41.2 reduce-scatter.19
  2406.5 280.2 reduce-scatter.17
  2689.0 282.0 reduce-scatter.13
where the time goes:
time: 3000 us; the launch traced here: 2990 us
  waiting for transfers between devices  1770 us (59%)
  matrix products  749 us (25%)
  other arithmetic  242 us (8%)
  local copies, waits for them, and re-layouts  119 us (4%)
  blocking collectives  69.5 us (2%)
    reduce_scatter x4, waiting for transfers between devices, sum_rows(): lax.psum_scatter(partial_rows, 'tensor', scatter_dimension=1, tiled=True)  1070 us
    all_gather x4, waiting for transfers between devices, gather_rows(): return lax.all_gather(local_rows, 'tensor', axis=1, tiled=True)  507 us
    dot_general x7, matrix products, matmul_nt(): lax.dot_general(left, right, (((1,), (1,)), ((), ())), preferred_element_...  123 us
    dot_general x8, matrix products, block_inputs(): jnp.einsum('qkgd,skd->kgqs', query_block, key_seq, preferred_element_type...  120 us
    convert_element_type x4, other arithmetic, one_block(): grad_score = (prob_rows * (grad_weights - row_dot)).astype(jnp.bfloat16)  115 us
    dot_general x7, matrix products, matmul(): return jnp.dot(left, right, preferred_element_type=jnp.float32)  107 us
    dot_general x4, matrix products, one_block(): jnp.einsum('qkgd,skd->kgqs', grad_block, value_seq, preferred_element_typ...  105 us
    dot_general x7, matrix products, matmul_tn(): lax.dot_general(left, right, (((0,), (0,)), ((), ())), preferred_element_...  104 us
  transfers between devices with their start and end apart: 20, of which 14 were waited for; matrix products, arithmetic and copies ran while one was open for 33% of the time, Pallas kernels for 0%

commit v1 on v0

--- a/solution.py
+++ b/solution.py
@@ -9,6 +9,19 @@
 QBLOCK = 512
 NORM_EPS = 1e-05
 ROPE_THETA = 500000.0
+
+
+def gather_around(x, axis, dim):
+    ways = lax.axis_size(axis)
+    up = [(d, (d + 1) % ways) for d in range(ways)]
+    down = [(d, (d - 1) % ways) for d in range(ways)]
+    earlier, later = ([x], [x])
+    for _ in range(ways // 2):
+        earlier.append(lax.ppermute(earlier[-1], axis, up))
+    for _ in range((ways - 1) // 2):
+        later.append(lax.ppermute(later[-1], axis, down))
+    line = jnp.concatenate([*earlier[::-1], *later[1:]], axis=dim)
+    return jnp.roll(line, (lax.axis_index(axis) - ways // 2) * x.shape[dim], axis=dim)
 
 
 def matmul(left, right):
@@ -84,7 +97,7 @@
 
 
 def gather_rows(local_rows):
-    return lax.all_gather(local_rows, "tensor", axis=1, tiled=True)
+    return gather_around(local_rows, "tensor", 1)
 
 
 def sum_rows(partial_rows):

time: 3000 us -> 2890 us (0.963)
  waiting for transfers between devices: 1770 us -> 1430 us
  other arithmetic: 242 us -> 391 us
  starting transfers between devices: 0.81 us -> 104 us
    all_gather x4 -> x0, waiting for transfers between devices: 507 us -> none  [gather_rows(): return lax.all_gather(local_rows, 'tensor', axis=1, tiled=True)]
    ppermute x0 -> x12, waiting for transfers between devices: none -> 311 us  [the longest x8 294 us: gather_around(): earlier.append(lax.ppermute(earlier[-1], axis, up))]
    reshape x0 -> x3, other arithmetic: none -> 123 us  [the longest x1 50.4 us: per_device(): gather_rows((resid * scale_two * mlp_gain).astype(jnp.bfloat16))]
    ppermute x0 -> x12, starting transfers between devices: none -> 104 us  [the longest x8 90.6 us: gather_around(): earlier.append(lax.ppermute(earlier[-1], axis, up))]
    all_gather x1, waiting for transfers between devices: 54.7 us -> 0.01 us  [per_device(): lax.all_gather(w_down, 'dp', axis=0, tiled=True)]
    all_gather x1, waiting for transfers between devices: 48.2 us -> 0.02 us  [per_device(): lax.all_gather(w_up, 'dp', axis=0, tiled=True)]
    all_gather x1, waiting for transfers between devices: 30.3 us -> 0.01 us  [per_device(): lax.all_gather(w_gate, 'dp', axis=0, tiled=True)]
  transfers between devices with their start and end apart: 20 -> 28, of which waited for: 14 -> 15; matrix products, arithmetic and copies ran while one was open for 33% -> 39% of each run, Pallas kernels for 0% -> 0%
where the time goes in v1:
time: 2890 us; the launch traced here: 2880 us
  waiting for transfers between devices  1430 us (49%)
  matrix products  735 us (25%)
  other arithmetic  391 us (14%)
  local copies, waits for them, and re-layouts  117 us (4%)
  starting transfers between devices  104 us (4%)
  blocking collectives  66.5 us (2%)
    reduce_scatter x4, waiting for transfers between devices, sum_rows(): lax.psum_scatter(partial_rows, 'tensor', scatter_dimension=1, tiled=True)  1060 us
    ppermute x8, waiting for transfers between devices, gather_around(): earlier.append(lax.ppermute(earlier[-1], axis, up))  294 us
    dot_general x7, matrix products, matmul_nt(): lax.dot_general(left, right, (((1,), (1,)), ((), ())), preferred_element_...  123 us
    dot_general x8, matrix products, block_inputs(): jnp.einsum('qkgd,skd->kgqs', query_block, key_seq, preferred_element_type...  116 us
    convert_element_type x4, other arithmetic, one_block(): grad_score = (prob_rows * (grad_weights - row_dot)).astype(jnp.bfloat16)  111 us
    dot_general x4, matrix products, one_block(): jnp.einsum('qkgd,skd->kgqs', grad_block, value_seq, preferred_element_typ...  105 us
    dot_general x7, matrix products, matmul_tn(): lax.dot_general(left, right, (((0,), (0,)), ((), ())), preferred_element_...  105 us
    dot_general x7, matrix products, matmul(): return jnp.dot(left, right, preferred_element_type=jnp.float32)  99.3 us
  transfers between devices with their start and end apart: 28, of which 15 were waited for; matrix products, arithmetic and copies ran while one was open for 39% of the time, Pallas kernels for 0%

profile of v1, /device:TPU:0, one launch (start us, length us, event | category | flops | bytes accessed | tf_op | source)
XLA Modules:
  0.0 2879.1 jit_solution(8493994120178935438)
XLA Ops:
  17.4 46.5 %collective-permute-done = bf16[1,512,2048]{2,1,0:T(8,128)(2,1)} collective-permute-done((bf16[1,512,2048]{2,1,0:T(8,128)(2,1)S(1)}, bf16[1,512,2048]{2,1,0:T(8,128)(2,1)}, u32[]{:S(2)}, u32[]{:S(2)}) %collective-permute-start) | collective-permute-done | bytes 2097184 | tf_op jit(solution)/shard_map/ppermute | solution.py:20
  107.6 45.3 %collective-permute-done.1 = bf16[1,512,2048]{2,1,0:T(8,128)(2,1)} collective-permute-done((bf16[1,512,2048]{2,1,0:T(8,128)(2,1)}, bf16[1,512,2048]{2,1,0:T(8,128)(2,1)}, u32[]{:S(2)}, u32[]{:S(2)}) %collective-permute-start.1) | collective-permute-done | bytes 2097184 | tf_op jit(solution)/shard_map/ppermute | solution.py:20
  153.0 29.2 %fusion.80 = bf16[1,2048,2048]{2,1,0:T(8,128)(2,1)S(1)} fusion(s32[]{:T(128)S(6)} %select_n.93, bf16[1,512,2048]{2,1,0:T(8,128)(2,1)} %collective-permute-done.1, bf16[1,512,2048]{2,1,0:T(8,128)(2,1)} %collective-permute-done, bf16[1,512,2048]{2,1,0:T(8,128)(2,1)S(1)} %fusion.98, bf16[1,512,2048]{2,1,0:T(8,128)(2,1)} %collective-permute-done.2), kind=kLoop, calls=%fused_computation.132 | loop fusion | flops 67108864 | bytes 16777220 | tf_op jit(solution)/shard_map/jit(_roll_dynamic)/concatenate | solution.py:24
  194.9 199.3 %while.30 = (s32[]{:T(128)}, bf16[4,512,2,4,64]{1,4,3,2,0:T(8,128)(2,1)}, f32[4,2,4,512]{3,2,1,0:T(4,128)}, s32[4]{0:T(128)S(1)}, s32[1,2048]{1,0:T(1,128)S(1)},...) while((s32[]{:T(128)}, ...), condition=%wide.region_6.8_spmd, body=%wide.region_3.7_spmd.sunk | while | flops 2251551232 | bytes 107104584 | solution.py:145
  414.2 317.5 %reduce-scatter.12.cloned.1.call-done = f32[1,512,2048]{2,1,0:T(8,128)} async-done(((f32[1,2048,2048]{2,1,0:T(8,128)}), f32[1,512,2048]{2,1,0:T(8,128)}) %reduce-scatter.12.cloned.1.call-update) | async-done | bytes 4194320 | tf_op jit(solution)/shard_map/reduce_scatter | solution.py:104
  744.8 42.7 %collective-permute-done.3 = bf16[1,512,2048]{2,1,0:T(8,128)(2,1)S(1)} collective-permute-done((bf16[1,512,2048]{2,1,0:T(8,128)(2,1)S(1)}, bf16[1,512,2048]{2,1,0:T(8,128)(2,1)S(1)}, u32[]{:S(2)}, u32[]{:S(2)}) %collective-permute-start.3) | collective-permute-done | bytes 2097184 | tf_op jit(solution)/shard_map/ppermute | solution.py:20
  787.5 43.6 %collective-permute-start.4 = (bf16[1,512,2048]{2,1,0:T(8,128)(2,1)S(1)}, bf16[1,512,2048]{2,1,0:T(8,128)(2,1)S(1)}, u32[]{:S(2)}, u32[]{:S(2)}) collective-permute-start(bf16[1,512,2048]{2,1,0:T(8,128)(2,1)S(1)} %collective-permute-done.3), channel_id=1, source_target_pairs={{0,1},{1,2},{2,3},{3,0},{4,5},{5,6},{6,7},{7,4},{8,9},{9,10},{10,1... | collective-permute-start | bytes 6291464 | tf_op jit(solution)/shard_map/ppermute | solution.py:20
  832.3 45.2 %collective-permute-done.7 = bf16[1,512,2048]{2,1,0:T(8,128)(2,1)S(1)} collective-permute-done((bf16[1,512,2048]{2,1,0:T(8,128)(2,1)}, bf16[1,512,2048]{2,1,0:T(8,128)(2,1)S(1)}, u32[]{:S(2)}, u32[]{:S(2)}) %collective-permute-start.7) | collective-permute-done | bytes 2097184 | tf_op jit(solution)/shard_map/ppermute | solution.py:20
  877.4 44.3 %fusion.65 = bf16[2048,2048]{1,0:T(8,128)(2,1)} fusion(s32[]{:T(128)S(6)} %select_n.93, bf16[1,512,2048]{2,1,0:T(8,128)(2,1)S(1)} %collective-permute-done.7, bf16[1,512,2048]{2,1,0:T(8,128)(2,1)} %collective-permute-done.6, bf16[1,512,2048]{2,1,0:T(8,128)(2,1)S(1)} %copy-done.11, bf16[1,512,2048]{2,1,0:T(8,128)(2,1)S(1)} %collective-permute-done.8), kind=kLoop, calls=%fused_computation.117 | loop fusion | flops 67108864 | bytes 16777220 | tf_op jit(solution)/shard_map/reshape | solution.py:269
  921.7 44.8 %collective-permute-done.4 = bf16[1,512,2048]{2,1,0:T(8,128)(2,1)S(1)} collective-permute-done((bf16[1,512,2048]{2,1,0:T(8,128)(2,1)S(1)}, bf16[1,512,2048]{2,1,0:T(8,128)(2,1)S(1)}, u32[]{:S(2)}, u32[]{:S(2)}) %collective-permute-start.4) | collective-permute-done | bytes 2097184 | tf_op jit(solution)/shard_map/ppermute | solution.py:20
  966.5 50.4 %fusion.73 = bf16[2048,2048]{1,0:T(8,128)(2,1)} fusion(s32[]{:T(128)S(6)} %select_n.93, bf16[1,512,2048]{2,1,0:T(8,128)(2,1)S(1)} %collective-permute-done.4, bf16[1,512,2048]{2,1,0:T(8,128)(2,1)S(1)} %collective-permute-done.3, bf16[1,512,2048]{2,1,0:T(8,128)(2,1)S(1)} %multiply_convert_fusion.3, bf16[1,512,2048]{2,1,0:T(8,128)(2,1)S(1)} %collective-permute-done.5), kind=kLoop, calls=%fused_computation.125 | loop fusion | flops 67108864 | bytes 16777220 | tf_op jit(solution)/shard_map/reshape | solution.py:255
  1065.3 34.8 %multiply_convert_fusion = (bf16[2048,2048]{1,0:T(8,128)(2,1)}, bf16[2048,2048]{1,0:T(8,128)(2,1)}, bf16[2048,2048]{1,0:T(8,128)(2,1)}) fusion(f32[2048,2048]{1,0:T(8,128)} %fusion.127, f32[2048,2048]{1,0:T(8,128)} %fusion.128, bf16[2048,2048]{1,0:T(8,128)(2,1)} %fusion.65, bf16[2048,2048]{1,0:T(8,128)(2,1)} %all-gather.14.cloned.1.call-done), kind=kOutput, calls=%fused_computation.99 | convolution fusion | flops 17246978048 | bytes 75497472 | tf_op jit(solution)/shard_map/dot_general | solution.py:28
  1199.1 231.2 %reduce-scatter.16.cloned.1.call-done = f32[1,512,2048]{2,1,0:T(8,128)} async-done(((f32[1,2048,2048]{2,1,0:T(8,128)}), f32[1,512,2048]{2,1,0:T(8,128)}) %reduce-scatter.16.cloned.1.call-update) | async-done | bytes 4194320 | tf_op jit(solution)/shard_map/reduce_scatter | solution.py:104
  1443.0 46.8 %collective-permute-done.9 = bf16[1,512,2048]{2,1,0:T(8,128)(2,1)S(1)} collective-permute-done((bf16[1,512,2048]{2,1,0:T(8,128)(2,1)}, bf16[1,512,2048]{2,1,0:T(8,128)(2,1)S(1)}, u32[]{:S(2)}, u32[]{:S(2)}) %collective-permute-start.9) | collective-permute-done | bytes 2097184 | tf_op jit(solution)/shard_map/ppermute | solution.py:20
  1489.8 43.3 %collective-permute-start.10 = (bf16[1,512,2048]{2,1,0:T(8,128)(2,1)S(1)}, bf16[1,512,2048]{2,1,0:T(8,128)(2,1)}, u32[]{:S(2)}, u32[]{:S(2)}) collective-permute-start(bf16[1,512,2048]{2,1,0:T(8,128)(2,1)S(1)} %collective-permute-done.9), channel_id=1, source_target_pairs={{0,1},{1,2},{2,3},{3,0},{4,5},{5,6},{6,7},{7,4},{8,9},{9,10},{10,1... | collective-permute-start | bytes 6291464 | tf_op jit(solution)/shard_map/ppermute | solution.py:20
  1579.8 28.2 fusion.57
  1613.9 510.6 %while.31 = (s32[]{:T(128)}, f32[4,512,2,4,64]{1,0,4,3,2:T(4,128)}, f32[4,2048,2,64]{1,3,2,0:T(8,128)}, f32[4,2048,2,64]{1,3,2,0:T(8,128)}, s32[4]{0:T(128)S(1)}...) while((s32[]{:T(128)}, f32[4,512,2,4,64]{1,0,4,3,2:T(4,128)}, ...), condition=%wide.region_14.16_spmd, body=%wide.region_12.15_spmd.sunk | while | flops 5498204672 | bytes 367659456 | solution.py:183
  1677.1 27.8 fusion.204
  1931.5 27.8 fusion.204
  2058.7 27.8 fusion.204
  2252.6 43.2 %reduce-scatter.20.cloned.1.call-done = bf16[256,512]{1,0:T(8,128)(2,1)} async-done(((bf16[2048,512]{1,0:T(8,128)(2,1)}), bf16[256,512]{1,0:T(8,128)(2,1)}) %reduce-scatter.20.cloned.1.call-update) | async-done | bytes 262160 | tf_op jit(solution)/shard_map/reduce_scatter | solution.py:319
  2297.5 280.9 %reduce-scatter.18.cloned.1.call-done = f32[1,512,2048]{2,1,0:T(8,128)} async-done(((f32[1,2048,2048]{2,1,0:T(8,128)}), f32[1,512,2048]{2,1,0:T(8,128)}) %reduce-scatter.18.cloned.1.call-update) | async-done | bytes 4194320 | tf_op jit(solution)/shard_map/reduce_scatter | solution.py:104
  2581.9 46.0 %all-reduce = (f32[2048]{0:T(1024)}, f32[2048]{0:T(1024)}) all-reduce(f32[2048]{0:T(1024)S(1)} %get-tuple-element.262, f32[2048]{0:T(1024)S(1)} %copy-done.41), channel_id=1, replica_groups=mesh['dp'=8,'tensor'=4] {'dp','tensor'}, use_global_device_ids=true, to_apply=%region_20.22 | all-reduce | flops 4096 | bytes 32768 | tf_op jit(solution)/shard_map/psum | solution.py:317
  2627.9 234.7 %reduce-scatter.14.cloned.1.call-done = f32[1,512,2048]{2,1,0:T(8,128)} async-done(((f32[1,2048,2048]{2,1,0:T(8,128)}), f32[1,512,2048]{2,1,0:T(8,128)}) %reduce-scatter.14.cloned.1.call-update) | async-done | bytes 4194320 | tf_op jit(solution)/shard_map/reduce_scatter | solution.py:104
  (316 shorter events, 1060.2 us)
Async XLA Ops:
  7.9 391.9 %all-gather.8.cloned.1.call-start = ((), (), s32[]{:S(2)}) async-start(), calls=%async_computation.12 | async-start | bytes 2359296 | tf_op jit(solution)/shard_map/all_gather | solution.py:219
  15.3 92.4 %collective-permute-start.2 = (bf16[1,512,2048]{2,1,0:T(8,128)(2,1)S(1)}, bf16[1,512,2048]{2,1,0:T(8,128)(2,1)}, u32[]{:S(2)}, u32[]{:S(2)}) collective-permute-start(bf16[1,512,2048]{2,1,0:T(8,128)(2,1)S(1)} %fusion.98), channel_id=1, source_target_pairs={{0,3},{1,0},{2,1},{3,2},{4,7},{5,4},{6,5},{7,6},{8,11},{9,8},{10,9... | collective-permute-start | bytes 6291464 | tf_op jit(solution)/shard_map/ppermute | solution.py:22
  63.9 89.0 %collective-permute-start.1 = (bf16[1,512,2048]{2,1,0:T(8,128)(2,1)}, bf16[1,512,2048]{2,1,0:T(8,128)(2,1)}, u32[]{:S(2)}, u32[]{:S(2)}) collective-permute-start(bf16[1,512,2048]{2,1,0:T(8,128)(2,1)} %collective-permute-done), channel_id=1, source_target_pairs={{0,1},{1,2},{2,3},{3,0},{4,5},{5,6},{6,7},{7,4},{8,9},{9,10},{10,1... | collective-permute-start | bytes 6291464 | tf_op jit(solution)/shard_map/ppermute | solution.py:20
  64.0 667.7 %reduce-scatter.12.cloned.1.call-start = ((), (), s32[]{:S(2)}) async-start(), calls=%async_computation.13 | async-start | bytes 20971520 | tf_op jit(solution)/shard_map/reduce_scatter | solution.py:104
  412.5 604.4 %all-gather.12.cloned.1.call-start = ((), (), s32[]{:S(2)}) async-start(), calls=%async_computation.15 | async-start | bytes 9437184 | tf_op jit(solution)/shard_map/all_gather | solution.py:251
  413.0 628.1 %all-gather.10.cloned.1.call-start = ((), (), s32[]{:S(2)}) async-start(), calls=%async_computation.14 | async-start | bytes 9437184 | tf_op jit(solution)/shard_map/all_gather | solution.py:250
  413.6 651.7 %all-gather.14.cloned.1.call-start = ((), (), s32[]{:S(2)}) async-start(), calls=%async_computation.16 | async-start | bytes 9437184 | tf_op jit(solution)/shard_map/all_gather | solution.py:252
  413.7 327.3 %collective-permute-start.6 = (bf16[1,512,2048]{2,1,0:T(8,128)(2,1)}, bf16[1,512,2048]{2,1,0:T(8,128)(2,1)}, u32[]{:S(2)}, u32[]{:S(2)}) collective-permute-start(bf16[1,512,2048]{2,1,0:T(8,128)(2,1)} %param.29), channel_id=1, source_target_pairs={{0,1},{1,2},{2,3},{3,0},{4,5},{5,6},{6,7},{7,4},{8,9},{9,10},{10,1... | collective-permute-start | bytes 6291464 | tf_op jit(solution)/shard_map/ppermute | solution.py:20
  414.2 1016.2 %reduce-scatter.16.cloned.1.call-start = ((), (), s32[]{:S(2)}) async-start(), calls=%async_computation.18 | async-start | bytes 20971520 | tf_op jit(solution)/shard_map/reduce_scatter | solution.py:104
  737.8 94.5 %collective-permute-start.8 = (bf16[1,512,2048]{2,1,0:T(8,128)(2,1)S(1)}, bf16[1,512,2048]{2,1,0:T(8,128)(2,1)S(1)}, u32[]{:S(2)}, u32[]{:S(2)}) collective-permute-start(bf16[1,512,2048]{2,1,0:T(8,128)(2,1)S(1)} %copy-done.11), channel_id=1, source_target_pairs={{0,3},{1,0},{2,1},{3,2},{4,7},{5,4},{6,5},{7,6},{8,11},{9,8},{10,9... | collective-permute-start | bytes 6291464 | tf_op jit(solution)/shard_map/ppermute | solution.py:22
  741.0 136.4 %collective-permute-start.7 = (bf16[1,512,2048]{2,1,0:T(8,128)(2,1)}, bf16[1,512,2048]{2,1,0:T(8,128)(2,1)S(1)}, u32[]{:S(2)}, u32[]{:S(2)}) collective-permute-start(bf16[1,512,2048]{2,1,0:T(8,128)(2,1)} %collective-permute-done.6), channel_id=1, source_target_pairs={{0,1},{1,2},{2,3},{3,0},{4,5},{5,6},{6,7},{7,4},{8,9},{9,10},{10,1... | collective-permute-start | bytes 6291464 | tf_op jit(solution)/shard_map/ppermute | solution.py:20
  741.0 180.7 %collective-permute-start.5 = (bf16[1,512,2048]{2,1,0:T(8,128)(2,1)S(1)}, bf16[1,512,2048]{2,1,0:T(8,128)(2,1)S(1)}, u32[]{:S(2)}, u32[]{:S(2)}) collective-permute-start(bf16[1,512,2048]{2,1,0:T(8,128)(2,1)S(1)} %multiply_convert_fusion.3), channel_id=1, source_target_pairs={{0,3},{1,0},{2,1},{3,2},{4,7},{5,4},{6,5},{7,6},{8,11},{9,8},{10,9... | collective-permute-start | bytes 6291464 | tf_op jit(solution)/shard_map/ppermute | solution.py:22
  787.5 179.0 %collective-permute-start.4 = (bf16[1,512,2048]{2,1,0:T(8,128)(2,1)S(1)}, bf16[1,512,2048]{2,1,0:T(8,128)(2,1)S(1)}, u32[]{:S(2)}, u32[]{:S(2)}) collective-permute-start(bf16[1,512,2048]{2,1,0:T(8,128)(2,1)S(1)} %collective-permute-done.3), channel_id=1, source_target_pairs={{0,1},{1,2},{2,3},{3,0},{4,5},{5,6},{6,7},{7,4},{8,9},{9,10},{10,1... | collective-permute-start | bytes 6291464 | tf_op jit(solution)/shard_map/ppermute | solution.py:20
  1150.9 1082.1 %reduce-scatter.32.cloned.1.call-start = ((), (), s32[]{:S(2)}) async-start(), calls=%async_computation.26 | async-start | bytes 9437184 | tf_op jit(solution)/shard_map/reduce_scatter | solution.py:337
  1174.7 1061.2 %reduce-scatter.30.cloned.1.call-start = ((), (), s32[]{:S(2)}) async-start(), calls=%async_computation.25 | async-start | bytes 9437184 | tf_op jit(solution)/shard_map/reduce_scatter | solution.py:334
  1199.1 1039.7 %reduce-scatter.28.cloned.1.call-start = ((), (), s32[]{:S(2)}) async-start(), calls=%async_computation.24 | async-start | bytes 9437184 | tf_op jit(solution)/shard_map/reduce_scatter | solution.py:331
  1439.2 118.4 %collective-permute-start.11 = (bf16[1,512,2048]{2,1,0:T(8,128)(2,1)}, bf16[1,512,2048]{2,1,0:T(8,128)(2,1)}, u32[]{:S(2)}, u32[]{:S(2)}) collective-permute-start(bf16[1,512,2048]{2,1,0:T(8,128)(2,1)} %fusion.126), channel_id=1, source_target_pairs={{0,3},{1,0},{2,1},{3,2},{4,7},{5,4},{6,5},{7,6},{8,11},{9,8},{10,9... | collective-permute-start | bytes 6291464 | tf_op jit(solution)/shard_map/ppermute | solution.py:22
  1489.8 90.0 %collective-permute-start.10 = (bf16[1,512,2048]{2,1,0:T(8,128)(2,1)S(1)}, bf16[1,512,2048]{2,1,0:T(8,128)(2,1)}, u32[]{:S(2)}, u32[]{:S(2)}) collective-permute-start(bf16[1,512,2048]{2,1,0:T(8,128)(2,1)S(1)} %collective-permute-done.9), channel_id=1, source_target_pairs={{0,1},{1,2},{2,3},{3,0},{4,5},{5,6},{6,7},{7,4},{8,9},{9,10},{10,1... | collective-permute-start | bytes 6291464 | tf_op jit(solution)/shard_map/ppermute | solution.py:20
  1557.5 684.1 %reduce-scatter.22.cloned.1.call-start = ((), (), s32[]{:S(2)}) async-start(), calls=%async_computation.21 | async-start | bytes 589824 | tf_op jit(solution)/shard_map/reduce_scatter | solution.py:322
  2134.0 109.1 %reduce-scatter.24.cloned.1.call-start = ((), (), s32[]{:S(2)}) async-start(), calls=%async_computation.22 | async-start | bytes 589824 | tf_op jit(solution)/shard_map/reduce_scatter | solution.py:325
  2143.3 107.5 %reduce-scatter.26.cloned.1.call-start = ((), (), s32[]{:S(2)}) async-start(), calls=%async_computation.23 | async-start | bytes 2359296 | tf_op jit(solution)/shard_map/reduce_scatter | solution.py:328
  2153.3 142.4 %reduce-scatter.20.cloned.1.call-start = ((), (), s32[]{:S(2)}) async-start(), calls=%async_computation.20 | async-start | bytes 2359296 | tf_op jit(solution)/shard_map/reduce_scatter | solution.py:319
  2173.6 404.8 %reduce-scatter.18.cloned.1.call-start = ((), (), s32[]{:S(2)}) async-start(), calls=%async_computation.19 | async-start | bytes 20971520 | tf_op jit(solution)/shard_map/reduce_scatter | solution.py:104
  2208.2 654.4 %reduce-scatter.14.cloned.1.call-start = ((), (), s32[]{:S(2)}) async-start(), calls=%async_computation.17 | async-start | bytes 20971520 | tf_op jit(solution)/shard_map/reduce_scatter | solution.py:104
  (58 other events, 6869.3 us)
Sparse Core Ops, SparseCore 0:
  9.9 30.5 all-gather.5
  64.1 70.9 all-gather.7
  412.6 319.1 reduce-scatter.11
  733.6 54.9 all-gather.11
  790.6 54.3 all-gather.9
  846.9 54.3 all-gather.13
  1151.0 279.2 reduce-scatter.15
  1433.8 71.9 reduce-scatter.31
  1509.7 71.2 reduce-scatter.29
  1584.3 71.2 reduce-scatter.27
  2134.1 33.4 reduce-scatter.21
  2171.1 34.1 reduce-scatter.23
  2209.5 41.2 reduce-scatter.25
  2254.5 41.2 reduce-scatter.19
  2298.1 280.2 reduce-scatter.17
  2580.6 281.9 reduce-scatter.13
